TPU v7x, 256 devices: a whole 4x4x8 slice. The times are simulated.
256 devices in a mesh: fsdp: 64 (over x, z, core), rep: 4 (over y).
Axes of the slice: x: 4, y: 4, z: 8, core: 2. Of those that a mesh axis runs over, the one named last changes fastest.
Arguments:
- grad: bfloat16 [128, 256, 2048], P(None, 'fsdp'), may hold values from -6 to 6
- momentum: float32 [128, 256, 2048], P(None, 'fsdp'), may hold values from -6 to 6
- owner_list: int32 [128], replicated, may hold values from 0 to 63, as said below
Outputs:
- new_momentum: float32 [128, 256, 2048], P(None, 'fsdp')
- update: bfloat16 [128, 256, 2048], P(None, 'fsdp')
- owned_update: bfloat16 [256, 256, 2048], P(('fsdp', 'rep'))
Inputs may be any that keep to these rules, and one draw needn't show every extreme that they name: `owner_list`: no owner is named by more than 4 matrices; some owner is named by exactly 4 in every draw.
All inputs are finite; a program needn't handle non-finite values.
Results may differ from a plain program's by a relative error of at most 0.03.
Values may be sent and summed in bfloat16 or wider, within the bound.
A program may use at most 128 MiB of HBM per device.

v0:
```python
import jax
import jax.numpy as jnp
from jax import lax
from jax.sharding import PartitionSpec as P

CAP = 4
ITERS = 5
decay_rate = 0.95
norm_eps = 1e-07
quintic_a = 3.4445
quintic_b = -4.775
quintic_c = 2.0315


def newton(blended):
    values = blended.astype(jnp.float32)
    total = jnp.sqrt(jnp.sum(values * values))
    current = (values / (total + norm_eps)).astype(jnp.bfloat16)
    for iteration in range(ITERS):
        gram = jnp.dot(current, current.T, preferred_element_type=jnp.float32).astype(jnp.bfloat16)
        square = jnp.dot(gram, gram, preferred_element_type=jnp.float32)
        poly = (quintic_b * gram.astype(jnp.float32) + quintic_c * square).astype(jnp.bfloat16)
        applied = jnp.dot(poly, current, preferred_element_type=jnp.float32)
        current = (quintic_a * current.astype(jnp.float32) + applied).astype(jnp.bfloat16)
    return current


def local(grad, momentum, owner_list):
    matrix_count, row_count, col_count = grad.shape
    owner_count = lax.axis_size("fsdp")
    replicas = lax.axis_size("rep")
    capacity = CAP
    per_replica = capacity // replicas
    replica = lax.axis_index("rep")
    new_momentum = decay_rate * momentum + grad.astype(jnp.float32)
    blended = (grad.astype(jnp.float32) + decay_rate * new_momentum).astype(jnp.bfloat16)
    order = jnp.arange(matrix_count)
    earlier = order[None, :] < order[:, None]
    same_owner = owner_list[None, :] == owner_list[:, None]
    slot_index = jnp.sum(jnp.logical_and(earlier, same_owner), axis=1)
    position = slot_index * owner_count + owner_list
    targets = jnp.arange(capacity * owner_count)
    matched = position[None, :] == targets[:, None]
    sources = jnp.sum(jnp.where(matched, order[None, :], 0), axis=1)
    filled = jnp.any(matched, axis=1)
    flattened = blended.reshape(matrix_count, row_count * col_count)
    first_slot = replica * per_replica
    chosen = lax.dynamic_slice_in_dim(sources, first_slot * owner_count, per_replica * owner_count)
    usable = lax.dynamic_slice_in_dim(filled, first_slot * owner_count, per_replica * owner_count)
    picked = jnp.take(flattened, chosen, axis=0)
    picked = jnp.where(usable[:, None], picked, jnp.zeros_like(picked))
    outgoing = picked.reshape(per_replica, owner_count, row_count, col_count)
    received = lax.all_to_all(outgoing, "fsdp", split_axis=1, concat_axis=1, tiled=True)
    items = received.shape[0]
    matrices = received.reshape(items, owner_count * row_count, col_count)
    result = jax.vmap(newton)(matrices)
    finished = result.reshape(items, owner_count, row_count, col_count)
    owned_update = finished.reshape(per_replica, owner_count * row_count, col_count)
    returned = lax.all_to_all(finished, "fsdp", split_axis=1, concat_axis=1, tiled=True)
    complete = lax.all_gather(returned, "rep", axis=0, tiled=True)
    stacked = complete.reshape(capacity * owner_count, row_count, col_count)
    update = jnp.take(stacked, position, axis=0)
    return (new_momentum, update, owned_update)


def solution(mesh):
    in_specs = (P(None, "fsdp", None), P(None, "fsdp", None), P())
    out_specs = (P(None, "fsdp", None), P(None, "fsdp", None), P(("fsdp", "rep"), None, None))
    return jax.shard_map(local, mesh=mesh, in_specs=in_specs, out_specs=out_specs, check_vma=False)
```

profile of v0, /device:TPU:1, one launch (start us, length us, event | category | flops | bytes accessed | tf_op | source)
XLA Modules:
  0.0 174.7 jit_solution(12986220659537661177)
XLA Ops:
  7.2 0.9 convert_reduce_fusion
  8.1 0.7 compare_and_fusion.1
  9.0 5.5 %fusion = (bf16[128,4,2048]{2,1,0:T(4,128)(2,1)S(1)}, f32[128,4,2048]{2,1,0:T(4,128)}) fusion(bf16[128,4,2048]{2,1,0:T(4,128)(2,1)} %param.3, f32[128,4,2048]{2,1,0:T(4,128)} %param.4), kind=kLoop, calls=%fused_computation.4 | loop fusion | flops 6291456 | bytes 12582912 | tf_op jit(solution)/shard_map/convert_element_type | solution.py:36
  14.6 1.4 copy.14
  16.1 1.2 gather_fusion
  17.3 0.8 gather.11
  18.2 0.7 fusion.18
  18.9 41.3 %all_to_all.10 = bf16[1,64,4,2048]{3,2,0,1:T(4,128)(2,1)S(1)} all-to-all(bf16[1,64,4,2048]{3,2,0,1:T(4,128)(2,1)S(1)} %fusion.18), channel_id=1, replica_groups=mesh['fsdp'=64,'rep'=4] {'fsdp'}, dimensions={1} | all-to-all | bytes 2097152 | tf_op jit(solution)/shard_map/all_to_all | solution.py:53
  60.2 1.7 fusion.6
  62.6 0.6 fusion.7
  64.0 0.6 fusion.1
  64.6 0.5 convolution_convert_fusion.3
  65.0 0.6 fusion.2
  66.1 0.6 fusion.3
  66.7 0.5 convolution_convert_fusion.1
  67.2 0.6 fusion.4
  67.7 0.5 convolution_convert_fusion
  68.2 0.6 fusion.5
  69.3 34.7 %all_to_all.11 = bf16[1,64,4,2048]{3,2,0,1:T(4,128)(2,1)S(1)} all-to-all(bf16[1,64,4,2048]{3,2,0,1:T(4,128)(2,1)S(1)} %bitcast.39), channel_id=1, replica_groups=mesh['fsdp'=64,'rep'=4] {'fsdp'}, dimensions={1} | all-to-all | bytes 2097152 | tf_op jit(solution)/shard_map/all_to_all | solution.py:59
  104.0 1.5 copy.12
  105.6 48.0 %all-gather.2.cloned.1.call-done = bf16[4,64,4,2048]{3,1,2,0:T(8,128)(2,1)} async-done(((bf16[1,64,4,2048]{3,1,2,0:T(8,128)(2,1)}), bf16[4,64,4,2048]{3,1,2,0:T(8,128)(2,1)}) %all-gather.2.cloned.1.call-update) | async-done | bytes 4194320 | tf_op jit(solution)/shard_map/all_gather | solution.py:60
  153.6 7.4 %copy.13 = bf16[4,64,4,2048]{3,2,1,0:T(4,128)(2,1)} copy(bf16[4,64,4,2048]{3,1,2,0:T(8,128)(2,1)} %all-gather.2.cloned.1.call-done) | data formatting | bytes 8388608 | tf_op jit(solution)/shard_map/all_gather | solution.py:60
  161.0 4.5 %gather_fusion.1 = bf16[128,4,2048]{2,1,0:T(4,128)(2,1)S(1)} fusion(bf16[256,4,2048]{2,1,0:T(4,128)(2,1)} %bitcast.37, s32[1024]{0:T(1024)S(1)} %pad_clamp_fusion), kind=kCustom, calls=%fused_computation.1 | custom fusion | bytes 4194816 | tf_op jit(solution)/shard_map/jit(_take)/gather | solution.py:62
  165.5 2.4 %broadcast_select_fusion = bf16[128,4,2048]{2,1,0:T(4,128)(2,1)} fusion(bf16[128,4,2048]{2,1,0:T(4,128)(2,1)S(1)} %gather_fusion.1, pred[128]{0:T(512)(128)(4,1)S(1)} %get-tuple-element.3), kind=kLoop, calls=%fused_computation.19 | loop fusion | flops 1048576 | bytes 4194432 | tf_op jit(solution)/shard_map/jit(_take)/select_n | solution.py:62
  (15 shorter events, 2.1 us)
Async XLA Ops:
  7.2 146.4 %all-gather.2.cloned.1.call-start = ((), (), s32[]{:S(2)}) async-start(), calls=%async_computation.2 | async-start | bytes 5242880 | tf_op jit(solution)/shard_map/all_gather | solution.py:60
  68.8 35.2 %copy-start = (bf16[256,2048]{1,0:T(8,128)(2,1)}, bf16[256,2048]{1,0:T(8,128)(2,1)S(1)}, u32[]{:S(2)}) copy-start(bf16[256,2048]{1,0:T(8,128)(2,1)S(1)} %fusion.5) | copy-start | bytes 3145732
Sparse Core Ops, SparseCore 0:
  105.7 47.8 all-gather.1
where the time goes:
time: 175 us
  blocking collectives  76.1 us (43%)
  waiting for transfers between devices  48 us (27%)
  local copies, waits for them, and re-layouts  17.7 us (10%)
  between operations  14.9 us (9%)
  other arithmetic  12.8 us (7%)
  matrix products  5.23 us (3%)
    all_gather x1, waiting for transfers between devices, local(): complete = lax.all_gather(returned, 'rep', axis=0, tiled=True)  48 us
    all_to_all x1, blocking collectives, local(): lax.all_to_all(outgoing, 'fsdp', split_axis=1, concat_axis=1, tiled=True)  41.3 us
    all_to_all x1, blocking collectives, local(): lax.all_to_all(finished, 'fsdp', split_axis=1, concat_axis=1, tiled=True)  34.7 us
    all_gather x1, local copies, waits for them, and re-layouts, local(): complete = lax.all_gather(returned, 'rep', axis=0, tiled=True)  7.43 us
    convert_element_type x1, other arithmetic, local(): (grad.astype(jnp.float32) + decay_rate * new_momentum).astype(jnp.bfloat16)  5.54 us
    gather x1, local copies, waits for them, and re-layouts, local(): update = jnp.take(stacked, position, axis=0)  4.52 us
  transfers between devices with their start and end apart: 1, of which 1 were waited for; matrix products, arithmetic and copies ran while one was open for 0% of the time, Pallas kernels for 0%

commit v1 on v0

--- a/solution.py
+++ b/solution.py
@@ -57,7 +57,9 @@
     finished = result.reshape(items, owner_count, row_count, col_count)
     owned_update = finished.reshape(per_replica, owner_count * row_count, col_count)
     returned = lax.all_to_all(finished, "fsdp", split_axis=1, concat_axis=1, tiled=True)
-    complete = lax.all_gather(returned, "rep", axis=0, tiled=True)
+    complete = jnp.concatenate(
+        lax.all_to_all(jnp.stack([returned] * lax.axis_size("rep")), "rep", 0, 0), axis=0
+    )
     stacked = complete.reshape(capacity * owner_count, row_count, col_count)
     update = jnp.take(stacked, position, axis=0)
     return (new_momentum, update, owned_update)

time: 175 us -> 163 us (0.931)
  between operations: 14.9 us -> 1.51 us
  starting transfers between devices: 0.04 us -> 4.86 us
  local copies, waits for them, and re-layouts: 17.7 us -> 12.9 us
    all_to_all x0 -> x1, waiting for transfers between devices: none -> 48.9 us  [local(): lax.all_to_all(jnp.stack([returned] * lax.axis_size('rep')), 'rep', 0, 0)]
    all_gather x1 -> x0, waiting for transfers between devices: 48 us -> none  [local(): complete = lax.all_gather(returned, 'rep', axis=0, tiled=True)]
    all_gather x1 -> x0, local copies, waits for them, and re-layouts: 7.43 us -> none  [local(): complete = lax.all_gather(returned, 'rep', axis=0, tiled=True)]
    all_to_all x0 -> x1, starting transfers between devices: none -> 4.86 us  [local(): lax.all_to_all(jnp.stack([returned] * lax.axis_size('rep')), 'rep', 0, 0)]
    another operation x0 -> x1, local copies, waits for them, and re-layouts: none -> 4.11 us  [local(): jnp.stack([returned] * lax.axis_size('rep'))]
where the time goes in v1:
time: 163 us; the launch traced here: 162 us
  blocking collectives  76.1 us (47%)
  waiting for transfers between devices  48.9 us (30%)
  local copies, waits for them, and re-layouts  12.9 us (8%)
  other arithmetic  12.8 us (8%)
  matrix products  5.23 us (3%)
  starting transfers between devices  4.86 us (3%)
    all_to_all x1, waiting for transfers between devices, local(): lax.all_to_all(jnp.stack([returned] * lax.axis_size('rep')), 'rep', 0, 0)  48.9 us
    all_to_all x1, blocking collectives, local(): lax.all_to_all(outgoing, 'fsdp', split_axis=1, concat_axis=1, tiled=True)  41.3 us
    all_to_all x1, blocking collectives, local(): lax.all_to_all(finished, 'fsdp', split_axis=1, concat_axis=1, tiled=True)  34.7 us
    convert_element_type x1, other arithmetic, local(): (grad.astype(jnp.float32) + decay_rate * new_momentum).astype(jnp.bfloat16)  5.54 us
    all_to_all x1, starting transfers between devices, local(): lax.all_to_all(jnp.stack([returned] * lax.axis_size('rep')), 'rep', 0, 0)  4.86 us
    gather x1, local copies, waits for them, and re-layouts, local(): update = jnp.take(stacked, position, axis=0)  4.52 us
    another operation x1, local copies, waits for them, and re-layouts, local(): jnp.stack([returned] * lax.axis_size('rep'))  4.11 us
  transfers between devices with their start and end apart: 1, of which 1 were waited for; matrix products, arithmetic and copies ran while one was open for 0% of the time, Pallas kernels for 0%

profile of v1, /device:TPU:1, one launch (start us, length us, event | category | flops | bytes accessed | tf_op | source)
XLA Modules:
  0.0 162.2 jit_solution(2913837613583305989)
XLA Ops:
  0.6 0.9 convert_reduce_fusion
  1.5 0.7 compare_and_fusion.1
  2.4 5.5 %fusion = (bf16[128,4,2048]{2,1,0:T(4,128)(2,1)S(1)}, f32[128,4,2048]{2,1,0:T(4,128)}) fusion(bf16[128,4,2048]{2,1,0:T(4,128)(2,1)} %param.3, f32[128,4,2048]{2,1,0:T(4,128)} %param.4), kind=kLoop, calls=%fused_computation.4 | loop fusion | flops 6291456 | bytes 12582912 | tf_op jit(solution)/shard_map/convert_element_type | solution.py:36
  8.0 1.4 copy.10
  9.5 1.2 gather_fusion
  10.7 0.8 gather.11
  11.6 0.7 fusion.18
  12.3 41.3 %all_to_all.18 = bf16[1,64,4,2048]{3,2,0,1:T(4,128)(2,1)S(1)} all-to-all(bf16[1,64,4,2048]{3,2,0,1:T(4,128)(2,1)S(1)} %fusion.18), channel_id=1, replica_groups=mesh['fsdp'=64,'rep'=4] {'fsdp'}, dimensions={1} | all-to-all | bytes 2097152 | tf_op jit(solution)/shard_map/all_to_all | solution.py:53
  53.7 1.7 %fusion.6 = f32[]{:T(128)} fusion(bf16[1,64,4,2048]{3,2,0,1:T(4,128)(2,1)S(1)} %all_to_all.18), kind=kLoop, calls=%fused_computation.17 | loop fusion | flops 1572863 | bytes 1048580 | tf_op jit(solution)/shard_map/vmap()/reduce_sum | solution.py:17
  56.0 0.6 fusion.7
  57.4 0.6 fusion.1
  58.5 0.6 fusion.2
  59.0 0.5 convolution_convert_fusion.2
  59.5 0.6 fusion.3
  60.1 0.5 convolution_convert_fusion.1
  60.6 0.6 fusion.4
  61.2 0.5 convolution_convert_fusion
  61.6 0.6 fusion.5
  62.7 34.7 %all_to_all.19 = bf16[1,64,4,2048]{3,2,0,1:T(4,128)(2,1)S(1)} all-to-all(bf16[1,64,4,2048]{3,2,0,1:T(4,128)(2,1)S(1)} %bitcast.40), channel_id=1, replica_groups=mesh['fsdp'=64,'rep'=4] {'fsdp'}, dimensions={1} | all-to-all | bytes 2097152 | tf_op jit(solution)/shard_map/all_to_all | solution.py:59
  97.4 4.1 %stack.2 = bf16[4,1,64,4,2048]{4,3,2,1,0:T(4,128)(2,1)} broadcast(bf16[64,4,2048]{2,1,0:T(4,128)(2,1)S(1)} %bitcast.39), dimensions={2,3,4} | broadcast | bytes 5242880 | tf_op jit(solution)/shard_map/stack | solution.py:61
  101.5 4.9 %all-to-all-start.2 = ((bf16[4,1,64,4,2048]{4,3,2,1,0:T(4,128)(2,1)}), bf16[4,1,64,4,2048]{4,3,2,1,0:T(4,128)(2,1)}, u32[]{:S(2)}, u32[]{:S(2)}) async-start(bf16[4,1,64,4,2048]{4,3,2,1,0:T(4,128)(2,1)} %stack.2), calls=%async_computation.2 | async-start | bytes 8388608 | tf_op jit(solution)/shard_map/all_to_all | solution.py:61
  106.4 48.9 %all-to-all-done.2 = bf16[4,1,64,4,2048]{4,3,2,1,0:T(4,128)(2,1)} async-done(((bf16[4,1,64,4,2048]{4,3,2,1,0:T(4,128)(2,1)}), bf16[4,1,64,4,2048]{4,3,2,1,0:T(4,128)(2,1)}, u32[]{:S(2)}, u32[]{:S(2)}) %all-to-all-start.2) | async-done | bytes 4194336 | tf_op jit(solution)/shard_map/all_to_all | solution.py:61
  155.3 4.5 %gather_fusion.1 = bf16[128,4,2048]{2,1,0:T(4,128)(2,1)S(1)} fusion(bf16[256,4,2048]{2,1,0:T(4,128)(2,1)} %bitcast.3, s32[1024]{0:T(1024)S(1)} %pad_clamp_fusion), kind=kCustom, calls=%fused_computation.1 | custom fusion | bytes 4194816 | tf_op jit(solution)/shard_map/jit(_take)/gather | solution.py:64
  159.9 2.4 %broadcast_select_fusion = bf16[128,4,2048]{2,1,0:T(4,128)(2,1)} fusion(bf16[128,4,2048]{2,1,0:T(4,128)(2,1)S(1)} %gather_fusion.1, pred[128]{0:T(512)(128)(4,1)S(1)} %get-tuple-element.3), kind=kLoop, calls=%fused_computation.19 | loop fusion | flops 1048576 | bytes 4194432 | tf_op jit(solution)/shard_map/jit(_take)/select_n | solution.py:64
  (13 shorter events, 2.1 us)
Async XLA Ops:
  62.2 35.2 %copy-start = (bf16[256,2048]{1,0:T(8,128)(2,1)}, bf16[256,2048]{1,0:T(8,128)(2,1)S(1)}, u32[]{:S(2)}) copy-start(bf16[256,2048]{1,0:T(8,128)(2,1)S(1)} %fusion.5) | copy-start | bytes 3145732
  101.5 53.8 %all-to-all-start.2 = ((bf16[4,1,64,4,2048]{4,3,2,1,0:T(4,128)(2,1)}), bf16[4,1,64,4,2048]{4,3,2,1,0:T(4,128)(2,1)}, u32[]{:S(2)}, u32[]{:S(2)}) async-start(bf16[4,1,64,4,2048]{4,3,2,1,0:T(4,128)(2,1)} %stack.2), calls=%async_computation.2 | async-start | bytes 8388608 | tf_op jit(solution)/shard_map/all_to_all | solution.py:61
